TPU v7x, 32 devices: a whole 2x2x4 slice. The times are simulated.
32 devices in a mesh: ka: 8 (over z, x), pt: 4 (over y, core).
Axes of the slice: x: 2, y: 2, z: 4, core: 2. Of those that a mesh axis runs over, the one named last changes fastest.
Arguments:
- wedge_orbitals: bfloat16 [2, 8, 4096, 128], P(None, 'ka', 'pt'), may hold values from -6 to 6
- star_members: int32 [8, 4], replicated, may hold values from -1 to 7, as said below
- star_ops: int32 [8, 4], replicated, may hold values from 0 to 47
- rotations: bfloat16 [48, 128, 128], replicated, may hold values from -0.5 to 0.5
- screen_left: bfloat16 [6, 4096, 64], P(None, 'pt'), may hold values from -2.5 to 2.5
- screen_right: bfloat16 [6, 4096, 64], P(None, 'pt'), may hold values from -2.5 to 2.5
Outputs:
- exchange_matrix: float32 [2, 8, 128, 128], P(None, 'ka', 'pt')
Inputs may be any that keep to these rules, and one draw needn't show every extreme that they name: `star_members`: every k-point 0 to 7 stands exactly once in the table; -1 marks an empty slot; the star of some wedge point fills all 4 slots.
All inputs are finite; a program needn't handle non-finite values.
Results may differ from a plain program's by a relative error of at most 0.0064.
Values may be sent and summed in bfloat16 or wider, within the bound.
No kernel may reach another device: no remote copies, remote signals or barrier semaphores. Data moves between devices by JAX's collectives and lax.ppermute only.
A program may use at most 128 MiB of HBM per device.

v0:
```python
import math
import jax
import jax.numpy as jnp
from jax import lax
from jax.sharding import PartitionSpec as P

NB = 128
NPTS = 4096
STOPS = 6
QBLK = 1024


def from_behind(block, axis, distance):
    devices = range(lax.axis_size(axis))
    route = [((i - distance) % len(devices), i) for i in devices]
    return lax.ppermute(block, axis, route)


def density_term(row_block, full_block, upper_half, lower_half, left_screen, right_screen):
    n_rows = row_block.shape[1]
    n_bands = row_block.shape[2]
    n_points = full_block.shape[1]
    left_rows = jnp.concatenate([row_block[0], row_block[1]], axis=1)
    swapped = jnp.concatenate([row_block[1], -row_block[0]], axis=1)
    stacked = jnp.concatenate([left_rows, swapped], axis=0)
    accum = jnp.zeros((n_rows, 2 * n_bands), jnp.float32)
    for column_block in range(n_points // QBLK):
        col_start = column_block * QBLK
        col_end = col_start + QBLK
        column_rows = jnp.concatenate(
            [full_block[0, col_start:col_end], full_block[1, col_start:col_end]], axis=1
        )
        density = lax.dot_general(
            stacked, column_rows, (((1,), (1,)), ((), ())), preferred_element_type=jnp.float32
        )
        screen_tile = lax.dot_general(
            left_screen,
            right_screen[col_start:col_end],
            (((1,), (1,)), ((), ())),
            preferred_element_type=jnp.float32,
        )
        real_part = (density[:n_rows] * screen_tile).astype(jnp.bfloat16)
        imag_part = (density[n_rows:] * screen_tile).astype(jnp.bfloat16)
        screened = jnp.concatenate([real_part, imag_part], axis=1)
        operand = jnp.concatenate(
            [upper_half[col_start:col_end], lower_half[col_start:col_end]], axis=0
        )
        accum = accum + jnp.dot(screened, operand, preferred_element_type=jnp.float32)
    return accum


def rotate_block(arrived, rotations, my_op):
    p_rows = arrived.shape[1]
    n_bands = arrived.shape[2]
    rotation = lax.dynamic_index_in_dim(rotations, my_op, 0, keepdims=False)
    product = jnp.dot(
        arrived.reshape(2 * p_rows, n_bands), rotation, preferred_element_type=jnp.float32
    )
    return product.astype(jnp.bfloat16).reshape(2, p_rows, n_bands)


def body(wedge_orbitals, star_members, star_ops, rotations, screen_left, screen_right):
    n_kpoints = lax.axis_size("ka")
    own_kpoint = lax.axis_index("ka")
    own_block = wedge_orbitals[:, 0]
    n_bands = own_block.shape[2]
    wedge_iota = jnp.arange(star_members.shape[0], dtype=jnp.int32)[:, None]
    located = star_members == own_kpoint
    wedge_source = jnp.sum(jnp.where(located, wedge_iota, 0))
    my_op = jnp.sum(jnp.where(located, star_ops, 0))
    my_star = lax.dynamic_index_in_dim(star_members, own_kpoint, 0, keepdims=False)
    target_iota = jnp.arange(n_kpoints, dtype=jnp.int32)
    wanted = jnp.any(my_star[None, :] == target_iota[:, None], axis=1)
    outgoing = jnp.where(
        wanted[:, None, None, None], own_block[None], jnp.zeros_like(own_block)[None]
    )
    incoming = lax.all_to_all(outgoing, "ka", split_axis=0, concat_axis=0, tiled=True)
    arrived = lax.dynamic_index_in_dim(incoming, wedge_source, 0, keepdims=False)
    rotated = rotate_block(arrived, rotations, my_op)
    full_block, right_all = (
        lax.all_gather(rotated, "pt", axis=1, tiled=True),
        lax.all_gather(screen_right, "pt", axis=1, tiled=True),
    )
    upper_half = jnp.concatenate([full_block[0], full_block[1]], axis=1)
    lower_half = jnp.concatenate([-full_block[1], full_block[0]], axis=1)
    lead_stops = STOPS // 2

    def stop_term(row_block, visited, stop):
        return density_term(
            row_block, visited, upper_half, lower_half, screen_left[stop], right_all[stop]
        )

    def gathered_rows(slice_rows):
        return lax.all_gather(slice_rows, "pt", axis=1, tiled=True)

    accum = stop_term(rotated, full_block, lead_stops)
    downward = rotated
    for stop in range(lead_stops + 1, STOPS):
        downward = from_behind(downward, "ka", 1)
        accum = accum + stop_term(downward, gathered_rows(downward), stop)
    upward = rotated
    for stop in range(lead_stops - 1, -1, -1):
        upward = from_behind(upward, "ka", -1)
        accum = accum + stop_term(upward, gathered_rows(upward), stop)
    rounded_y = accum.astype(jnp.bfloat16)
    y_real = rounded_y[:, :n_bands]
    y_imag = rounded_y[:, n_bands:]
    stacked_x = jnp.concatenate([rotated[0], rotated[1]], axis=0)
    right_stack = jnp.concatenate([rounded_y, jnp.concatenate([y_imag, -y_real], axis=1)], axis=0)
    partial_value = lax.dot_general(
        stacked_x, right_stack, (((0,), (0,)), ((), ())), preferred_element_type=jnp.float32
    )
    rows_out = n_bands // lax.axis_size("pt")
    summed = lax.psum(partial_value, "pt")
    kept = lax.dynamic_slice_in_dim(summed, lax.axis_index("pt") * rows_out, rows_out, 0)
    scale_factor = 1.0 / (4.0 * NPTS * math.sqrt(NB))
    kept = kept * scale_factor
    return jnp.stack([kept[:, :n_bands], kept[:, n_bands:]])[:, None]


def solution(mesh):
    return jax.shard_map(
        body,
        mesh=mesh,
        in_specs=(
            P(None, "ka", "pt", None),
            P(),
            P(),
            P(),
            P(None, "pt", None),
            P(None, "pt", None),
        ),
        out_specs=P(None, "ka", "pt", None),
        check_vma=False,
    )
```

profile of v0, /device:TPU:0, one launch (start us, length us, event | category | flops | bytes accessed | tf_op | source)
XLA Modules:
  0.0 436.4 jit_solution(8135102432398648651)
XLA Ops:
  11.1 7.4 %all-to-all-start = ((bf16[8,2,1024,128]{3,2,1,0:T(8,128)(2,1)}), bf16[8,2,1024,128]{3,2,1,0:T(8,128)(2,1)}, u32[]{:S(2)}, u32[]{:S(2)}) async-start(bf16[8,2,1024,128]{3,2,1,0:T(8,128)(2,1)} %broadcast_select_fusion), calls=%async_computation | async-start | bytes 8388608 | tf_op jit(solution)/shard_map/all_to_all | solution.py:77
  23.3 88.6 %all-to-all-done = bf16[8,2,1024,128]{3,2,1,0:T(8,128)(2,1)} async-done(((bf16[8,2,1024,128]{3,2,1,0:T(8,128)(2,1)}), bf16[8,2,1024,128]{3,2,1,0:T(8,128)(2,1)}, u32[]{:S(2)}, u32[]{:S(2)}) %all-to-all-start) | async-done | bytes 4194336 | tf_op jit(solution)/shard_map/all_to_all | solution.py:77
  116.4 14.0 %collective-permute-done = bf16[2,1024,128]{2,1,0:T(8,128)(2,1)S(1)} collective-permute-done((bf16[2,1024,128]{2,1,0:T(8,128)(2,1)}, bf16[2,1024,128]{2,1,0:T(8,128)(2,1)S(1)}, u32[]{:S(2)}, u32[]{:S(2)}) %collective-permute-start) | collective-permute-done | bytes 524320 | tf_op jit(solution)/shard_map/ppermute | solution.py:16
  132.2 11.0 %collective-permute-done.2 = bf16[2,1024,128]{2,1,0:T(8,128)(2,1)S(1)} collective-permute-done((bf16[2,1024,128]{2,1,0:T(8,128)(2,1)}, bf16[2,1024,128]{2,1,0:T(8,128)(2,1)S(1)}, u32[]{:S(2)}, u32[]{:S(2)}) %collective-permute-start.2) | collective-permute-done | bytes 524320 | tf_op jit(solution)/shard_map/ppermute | solution.py:16
  144.7 15.2 %collective-permute-done.1 = bf16[2,1024,128]{2,1,0:T(8,128)(2,1)S(1)} collective-permute-done((bf16[2,1024,128]{2,1,0:T(8,128)(2,1)}, bf16[2,1024,128]{2,1,0:T(8,128)(2,1)S(1)}, u32[]{:S(2)}, u32[]{:S(2)}) %collective-permute-start.1) | collective-permute-done | bytes 524320 | tf_op jit(solution)/shard_map/ppermute | solution.py:16
  162.6 10.1 %collective-permute-done.3 = bf16[2,1024,128]{2,1,0:T(8,128)(2,1)S(1)} collective-permute-done((bf16[2,1024,128]{2,1,0:T(8,128)(2,1)}, bf16[2,1024,128]{2,1,0:T(8,128)(2,1)S(1)}, u32[]{:S(2)}, u32[]{:S(2)}) %collective-permute-start.3) | collective-permute-done | bytes 524320 | tf_op jit(solution)/shard_map/ppermute | solution.py:16
  182.4 6.4 %collective-permute-done.4 = bf16[2,1024,128]{2,1,0:T(8,128)(2,1)S(1)} collective-permute-done((bf16[2,1024,128]{2,1,0:T(8,128)(2,1)S(1)}, bf16[2,1024,128]{2,1,0:T(8,128)(2,1)S(1)}, u32[]{:S(2)}, u32[]{:S(2)}) %collective-permute-start.4) | collective-permute-done | bytes 524320 | tf_op jit(solution)/shard_map/ppermute | solution.py:16
  196.5 4.7 %fusion.232 = f32[2048,1024]{0,1:T(8,128)} fusion(bf16[1024,128]{1,0:T(8,128)(2,1)S(1)} %get-tuple-element.101, bf16[1024,128]{1,0:T(8,128)(2,1)S(1)} %get-tuple-element.102, bf16[1024,128]{1,0:T(8,128)(2,1)S(1)} %get-tuple-element.127, bf16[1024,128]{1,0:T(8,128)(2,1)S(1)} %get-tuple-element.128, bf16[1024,128]{1,0:T(8,128)(2,1)S(1)} %get-tuple-element.126), kind=kOutput, calls=%fused_computation.259 | convolution fusion | flops 1078984704 | bytes 9699328 | tf_op jit(solution)/shard_map/dot_general | solution.py:33
  201.1 4.6 %fusion.236 = f32[2048,1024]{0,1:T(8,128)} fusion(bf16[1024,128]{1,0:T(8,128)(2,1)S(1)} %get-tuple-element.99, bf16[1024,128]{1,0:T(8,128)(2,1)S(1)} %get-tuple-element.100, bf16[1024,128]{1,0:T(8,128)(2,1)S(1)} %get-tuple-element.127, bf16[1024,128]{1,0:T(8,128)(2,1)S(1)} %get-tuple-element.128, bf16[1024,128]{1,0:T(8,128)(2,1)S(1)} %get-tuple-element.126), kind=kOutput, calls=%fused_computation.263 | convolution fusion | flops 1078984704 | bytes 9699328 | tf_op jit(solution)/shard_map/dot_general | solution.py:33
  205.7 4.7 %fusion.240 = f32[2048,1024]{0,1:T(8,128)} fusion(bf16[1024,128]{1,0:T(8,128)(2,1)S(1)} %get-tuple-element.97, bf16[1024,128]{1,0:T(8,128)(2,1)S(1)} %get-tuple-element.98, bf16[1024,128]{1,0:T(8,128)(2,1)S(1)} %get-tuple-element.127, bf16[1024,128]{1,0:T(8,128)(2,1)S(1)} %get-tuple-element.128, bf16[1024,128]{1,0:T(8,128)(2,1)S(1)} %get-tuple-element.126), kind=kOutput, calls=%fused_computation.267 | convolution fusion | flops 1078984704 | bytes 9699328 | tf_op jit(solution)/shard_map/dot_general | solution.py:33
  210.4 4.6 %fusion.244 = f32[2048,1024]{0,1:T(8,128)} fusion(bf16[1024,128]{1,0:T(8,128)(2,1)S(1)} %get-tuple-element.96, bf16[1024,128]{1,0:T(8,128)(2,1)S(1)} %get-tuple-element.95, bf16[1024,128]{1,0:T(8,128)(2,1)S(1)} %get-tuple-element.127, bf16[1024,128]{1,0:T(8,128)(2,1)S(1)} %get-tuple-element.128, bf16[1024,128]{1,0:T(8,128)(2,1)S(1)} %get-tuple-element.126), kind=kOutput, calls=%fused_computation.271 | convolution fusion | flops 1078984704 | bytes 9699328 | tf_op jit(solution)/shard_map/dot_general | solution.py:33
  215.0 4.4 %fusion.47 = (bf16[1024,1024]{0,1:T(8,128)(2,1)S(1)}, bf16[1024,1024]{0,1:T(8,128)(2,1)S(1)}) fusion(f32[2048,1024]{0,1:T(8,128)} %fusion.232, bf16[6,4096,64]{1,2,0:T(8,128)(2,1)} %all-gather.10.cloned.1.call-done, bf16[6,1024,64]{1,2,0:T(8,128)(2,1)S(1)} %copy-done.3), kind=kOutput, calls=%fused_computation.95 | convolution fusion | flops 138412032 | bytes 12845056 | tf_op jit(solution)/shard_map/dot_general | solution.py:36
  241.9 4.7 %fusion.252 = f32[2048,1024]{0,1:T(8,128)} fusion(bf16[1024,128]{1,0:T(8,128)(2,1)S(1)} %get-tuple-element.91, bf16[1024,128]{1,0:T(8,128)(2,1)S(1)} %get-tuple-element.92, bf16[1024,128]{1,0:T(8,128)(2,1)S(1)} %fusion.453, bf16[1024,128]{1,0:T(8,128)(2,1)S(1)} %copy-done.14, bf16[1024,128]{1,0:T(8,128)(2,1)S(1)} %copy-done.13), kind=kOutput, calls=%fused_computation.279 | convolution fusion | flops 1078984704 | bytes 9699328 | tf_op jit(solution)/shard_map/dot_general | solution.py:33
  246.6 4.6 %fusion.256 = f32[2048,1024]{0,1:T(8,128)} fusion(bf16[1024,128]{1,0:T(8,128)(2,1)S(1)} %get-tuple-element.89, bf16[1024,128]{1,0:T(8,128)(2,1)S(1)} %get-tuple-element.90, bf16[1024,128]{1,0:T(8,128)(2,1)S(1)} %fusion.453, bf16[1024,128]{1,0:T(8,128)(2,1)S(1)} %copy-done.14, bf16[1024,128]{1,0:T(8,128)(2,1)S(1)} %copy-done.13), kind=kOutput, calls=%fused_computation.283 | convolution fusion | flops 1078984704 | bytes 9699328 | tf_op jit(solution)/shard_map/dot_general | solution.py:33
  251.2 4.7 %fusion.260 = f32[2048,1024]{0,1:T(8,128)} fusion(bf16[1024,128]{1,0:T(8,128)(2,1)S(1)} %get-tuple-element.88, bf16[1024,128]{1,0:T(8,128)(2,1)S(1)} %get-tuple-element.87, bf16[1024,128]{1,0:T(8,128)(2,1)S(1)} %fusion.453, bf16[1024,128]{1,0:T(8,128)(2,1)S(1)} %copy-done.14, bf16[1024,128]{1,0:T(8,128)(2,1)S(1)} %copy-done.13), kind=kOutput, calls=%fused_computation.287 | convolution fusion | flops 1078984704 | bytes 9699328 | tf_op jit(solution)/shard_map/dot_general | solution.py:33
  272.1 5.2 %fusion.203 = f32[1024,256]{1,0:T(8,128)} fusion(f32[1024,256]{1,0:T(8,128)} %fusion.64, bf16[1024,1024]{0,1:T(8,128)(2,1)} %get-tuple-element.44, bf16[1024,1024]{0,1:T(8,128)(2,1)} %get-tuple-element.43, bf16[1024,256]{1,0:T(8,128)(2,1)} %get-tuple-element.111, bf16[1024,256]{1,0:T(8,128)(2,1)} %get-tuple-element.105), kind=kOutput, calls=%fused_computation.228 | convolution fusion | flops 1084489728 | bytes 7340032 | tf_op jit(solution)/shard_map/dot_general | solution.py:48
  304.5 4.6 %fusion.268 = f32[2048,1024]{0,1:T(8,128)} fusion(bf16[1024,128]{1,0:T(8,128)(2,1)S(1)} %get-tuple-element.83, bf16[1024,128]{1,0:T(8,128)(2,1)S(1)} %get-tuple-element.84, bf16[1024,128]{1,0:T(8,128)(2,1)S(1)} %fusion.454, bf16[1024,128]{1,0:T(8,128)(2,1)S(1)} %copy-done.9, bf16[1024,128]{1,0:T(8,128)(2,1)S(1)} %copy-done.8), kind=kOutput, calls=%fused_computation.295 | convolution fusion | flops 1078984704 | bytes 9699328 | tf_op jit(solution)/shard_map/dot_general | solution.py:33
  309.1 4.7 %fusion.272 = f32[2048,1024]{0,1:T(8,128)} fusion(bf16[1024,128]{1,0:T(8,128)(2,1)S(1)} %get-tuple-element.81, bf16[1024,128]{1,0:T(8,128)(2,1)S(1)} %get-tuple-element.82, bf16[1024,128]{1,0:T(8,128)(2,1)S(1)} %fusion.454, bf16[1024,128]{1,0:T(8,128)(2,1)S(1)} %copy-done.9, bf16[1024,128]{1,0:T(8,128)(2,1)S(1)} %copy-done.8), kind=kOutput, calls=%fused_computation.299 | convolution fusion | flops 1078984704 | bytes 9699328 | tf_op jit(solution)/shard_map/dot_general | solution.py:33
  313.8 4.6 %fusion.276 = f32[2048,1024]{0,1:T(8,128)} fusion(bf16[1024,128]{1,0:T(8,128)(2,1)S(1)} %get-tuple-element.80, bf16[1024,128]{1,0:T(8,128)(2,1)S(1)} %get-tuple-element.79, bf16[1024,128]{1,0:T(8,128)(2,1)S(1)} %fusion.454, bf16[1024,128]{1,0:T(8,128)(2,1)S(1)} %copy-done.9, bf16[1024,128]{1,0:T(8,128)(2,1)S(1)} %copy-done.8), kind=kOutput, calls=%fused_computation.303 | convolution fusion | flops 1078984704 | bytes 9699328 | tf_op jit(solution)/shard_map/dot_general | solution.py:33
  320.1 4.7 %fusion.296 = f32[2048,1024]{0,1:T(8,128)} fusion(bf16[1024,128]{1,0:T(8,128)(2,1)S(1)} %get-tuple-element.69, bf16[1024,128]{1,0:T(8,128)(2,1)S(1)} %get-tuple-element.70, bf16[1024,128]{1,0:T(8,128)(2,1)S(1)} %fusion.456, bf16[1024,128]{1,0:T(8,128)(2,1)S(1)} %copy-done.7, bf16[1024,128]{1,0:T(8,128)(2,1)S(1)} %get-tuple-element.118), kind=kOutput, calls=%fused_computation.323 | convolution fusion | flops 1078984704 | bytes 9699328 | tf_op jit(solution)/shard_map/dot_general | solution.py:33
  324.8 4.7 %fusion.300 = f32[2048,1024]{0,1:T(8,128)} fusion(bf16[1024,128]{1,0:T(8,128)(2,1)S(1)} %get-tuple-element.67, bf16[1024,128]{1,0:T(8,128)(2,1)S(1)} %get-tuple-element.68, bf16[1024,128]{1,0:T(8,128)(2,1)S(1)} %fusion.456, bf16[1024,128]{1,0:T(8,128)(2,1)S(1)} %copy-done.7, bf16[1024,128]{1,0:T(8,128)(2,1)S(1)} %get-tuple-element.118), kind=kOutput, calls=%fused_computation.327 | convolution fusion | flops 1078984704 | bytes 9699328 | tf_op jit(solution)/shard_map/dot_general | solution.py:33
  337.2 5.2 %fusion.191 = f32[1024,256]{1,0:T(8,128)} fusion(f32[1024,256]{1,0:T(8,128)} %fusion.80, bf16[1024,1024]{0,1:T(8,128)(2,1)} %get-tuple-element.36, bf16[1024,1024]{0,1:T(8,128)(2,1)} %get-tuple-element.35, bf16[1024,256]{1,0:T(8,128)(2,1)} %get-tuple-element.111, bf16[1024,256]{1,0:T(8,128)(2,1)} %get-tuple-element.105), kind=kOutput, calls=%fused_computation.224 | convolution fusion | flops 1084489728 | bytes 7340032 | tf_op jit(solution)/shard_map/dot_general | solution.py:48
  345.9 6.4 %fusion.15 = (bf16[1024,1024]{0,1:T(8,128)(2,1)}, bf16[1024,1024]{0,1:T(8,128)(2,1)}) fusion(f32[2048,1024]{0,1:T(8,128)} %fusion.296, bf16[6,4096,64]{1,2,0:T(8,128)(2,1)} %all-gather.10.cloned.1.call-done, bf16[6,1024,64]{1,2,0:T(8,128)(2,1)S(1)} %copy-done.3), kind=kOutput, calls=%fused_computation.31 | convolution fusion | flops 138412032 | bytes 12845056 | tf_op jit(solution)/shard_map/dot_general | solution.py:36
  394.0 33.9 %all-reduce.2.cloned.1.call-done = f32[128,256]{1,0:T(8,128)} async-done(((f32[128,256]{1,0:T(8,128)}), f32[128,256]{1,0:T(8,128)}) %all-reduce.2.cloned.1.call-update) | async-done | bytes 131088 | tf_op jit(solution)/shard_map/psum | solution.py:114
  (308 shorter events, 153.8 us)
Async XLA Ops:
  6.5 106.4 %copy-start = (bf16[48,128,128]{2,1,0:T(8,128)(2,1)S(1)}, bf16[48,128,128]{2,1,0:T(8,128)(2,1)}, u32[]{:S(2)}) copy-start(bf16[48,128,128]{2,1,0:T(8,128)(2,1)} %param.9) | copy-start | bytes 4718596
  11.1 7.5 %copy-start.64 = (s32[8,4]{0,1:T(4,128)S(1)}, s32[8,4]{0,1:T(4,128)}, u32[]{:S(2)}) copy-start(s32[8,4]{0,1:T(4,128)} %param.8) | copy-start | bytes 388
  11.1 100.7 %all-to-all-start = ((bf16[8,2,1024,128]{3,2,1,0:T(8,128)(2,1)}), bf16[8,2,1024,128]{3,2,1,0:T(8,128)(2,1)}, u32[]{:S(2)}, u32[]{:S(2)}) async-start(bf16[8,2,1024,128]{3,2,1,0:T(8,128)(2,1)} %broadcast_select_fusion), calls=%async_computation | async-start | bytes 8388608 | tf_op jit(solution)/shard_map/all_to_all | solution.py:77
  18.6 172.0 %all-gather.8.cloned.1.call-start = ((), (), s32[]{:S(2)}) async-start(), calls=%async_computation.1 | async-start | bytes 2621440 | tf_op jit(solution)/shard_map/all_gather | solution.py:81
  114.0 59.6 %copy-start.15 = (bf16[2048,128]{1,0:T(8,128)(2,1)S(1)}, bf16[2048,128]{1,0:T(8,128)(2,1)}, u32[]{:S(2)}) copy-start(bf16[2048,128]{1,0:T(8,128)(2,1)} %convolution_convert_fusion) | copy-start | bytes 1572868
  114.1 100.9 %all-gather.10.cloned.1.call-start = ((), (), s32[]{:S(2)}) async-start(), calls=%async_computation.2 | async-start | bytes 3932160 | tf_op jit(solution)/shard_map/all_gather | solution.py:82
  114.8 120.0 %all-gather.12.cloned.1.call-start = ((), (), s32[]{:S(2)}) async-start(), calls=%async_computation.3 | async-start | bytes 2621440 | tf_op jit(solution)/shard_map/all_gather | solution.py:94
  114.9 15.5 %collective-permute-start = (bf16[2,1024,128]{2,1,0:T(8,128)(2,1)}, bf16[2,1024,128]{2,1,0:T(8,128)(2,1)S(1)}, u32[]{:S(2)}, u32[]{:S(2)}) collective-permute-start(bf16[2,1024,128]{2,1,0:T(8,128)(2,1)} %bitcast.397), channel_id=1, source_target_pairs={{28,0},{0,4},{4,8},{8,12},{12,16},{16,20},{20,24},{24,28},{29,1},{... | collective-permute-start | bytes 1572872 | tf_op jit(solution)/shard_map/ppermute | solution.py:16
  131.2 42.5 %copy-start.25 = (bf16[2,1024,128]{2,1,0:T(8,128)(2,1)S(1)}, bf16[2,1024,128]{2,1,0:T(8,128)(2,1)}, u32[]{:S(2)}) copy-start(bf16[2,1024,128]{2,1,0:T(8,128)(2,1)} %copy-done.24) | copy-start | bytes 1572868
  131.2 124.6 %all-gather.16.cloned.1.call-start = ((), (), s32[]{:S(2)}) async-start(), calls=%async_computation.5 | async-start | bytes 2621440 | tf_op jit(solution)/shard_map/all_gather | solution.py:94
  131.3 12.0 %collective-permute-start.2 = (bf16[2,1024,128]{2,1,0:T(8,128)(2,1)}, bf16[2,1024,128]{2,1,0:T(8,128)(2,1)S(1)}, u32[]{:S(2)}, u32[]{:S(2)}) collective-permute-start(bf16[2,1024,128]{2,1,0:T(8,128)(2,1)} %bitcast.398), channel_id=1, source_target_pairs={{4,0},{8,4},{12,8},{16,12},{20,16},{24,20},{28,24},{0,28},{5,1},{9... | collective-permute-start | bytes 1572872 | tf_op jit(solution)/shard_map/ppermute | solution.py:16
  144.1 29.7 %copy-start.23 = (bf16[2,1024,128]{2,1,0:T(8,128)(2,1)S(1)}, bf16[2,1024,128]{2,1,0:T(8,128)(2,1)}, u32[]{:S(2)}) copy-start(bf16[2,1024,128]{2,1,0:T(8,128)(2,1)} %copy-done.22) | copy-start | bytes 1572868
  144.1 153.3 %all-gather.14.cloned.1.call-start = ((), (), s32[]{:S(2)}) async-start(), calls=%async_computation.4 | async-start | bytes 2621440 | tf_op jit(solution)/shard_map/all_gather | solution.py:94
  144.2 15.7 %collective-permute-start.1 = (bf16[2,1024,128]{2,1,0:T(8,128)(2,1)}, bf16[2,1024,128]{2,1,0:T(8,128)(2,1)S(1)}, u32[]{:S(2)}, u32[]{:S(2)}) collective-permute-start(bf16[2,1024,128]{2,1,0:T(8,128)(2,1)} %copy-done.24), channel_id=1, source_target_pairs={{28,0},{0,4},{4,8},{8,12},{12,16},{16,20},{20,24},{24,28},{29,1},{... | collective-permute-start | bytes 1572872 | tf_op jit(solution)/shard_map/ppermute | solution.py:16
  160.7 157.7 %all-gather.18.cloned.1.call-start = ((), (), s32[]{:S(2)}) async-start(), calls=%async_computation.6 | async-start | bytes 2621440 | tf_op jit(solution)/shard_map/all_gather | solution.py:94
  160.8 11.9 %collective-permute-start.3 = (bf16[2,1024,128]{2,1,0:T(8,128)(2,1)}, bf16[2,1024,128]{2,1,0:T(8,128)(2,1)S(1)}, u32[]{:S(2)}, u32[]{:S(2)}) collective-permute-start(bf16[2,1024,128]{2,1,0:T(8,128)(2,1)} %copy-done.22), channel_id=1, source_target_pairs={{4,0},{8,4},{12,8},{16,12},{20,16},{24,20},{28,24},{0,28},{5,1},{9... | collective-permute-start | bytes 1572872 | tf_op jit(solution)/shard_map/ppermute | solution.py:16
  173.6 199.8 %all-gather.20.cloned.1.call-start = ((), (), s32[]{:S(2)}) async-start(), calls=%async_computation.7 | async-start | bytes 2621440 | tf_op jit(solution)/shard_map/all_gather | solution.py:94
  176.4 12.3 %collective-permute-start.4 = (bf16[2,1024,128]{2,1,0:T(8,128)(2,1)S(1)}, bf16[2,1024,128]{2,1,0:T(8,128)(2,1)S(1)}, u32[]{:S(2)}, u32[]{:S(2)}) collective-permute-start(bf16[2,1024,128]{2,1,0:T(8,128)(2,1)S(1)} %copy-done.19), channel_id=1, source_target_pairs={{4,0},{8,4},{12,8},{16,12},{20,16},{24,20},{28,24},{0,28},{5,1},{9... | collective-permute-start | bytes 1572872 | tf_op jit(solution)/shard_map/ppermute | solution.py:16
  190.4 237.4 %all-reduce.2.cloned.1.call-start = ((), (), s32[]{:S(2)}) async-start(), calls=%async_computation.8 | async-start | bytes 262144 | tf_op jit(solution)/shard_map/psum | solution.py:114
  268.2 9.1 %slice-start.2 = ((s8[8388608]{0:T(1024)(128)(4,1)}), s8[4194304]{0:T(1024)(128)(4,1)S(1)}, s32[]{:S(2)}) async-start(s8[8388608]{0:T(1024)(128)(4,1)} %bitcast.378), calls=%async_computation.11 | async-start | bytes 8388608
  333.2 9.2 %slice-start.6 = ((s8[8388608]{0:T(1024)(128)(4,1)}), s8[4194304]{0:T(1024)(128)(4,1)S(1)}, s32[]{:S(2)}) async-start(s8[8388608]{0:T(1024)(128)(4,1)} %bitcast.382), calls=%async_computation.15 | async-start | bytes 8388608
  333.2 10.8 %slice-start.8 = ((s8[8388608]{0:T(1024)(128)(4,1)}), s8[4194304]{0:T(1024)(128)(4,1)S(1)}, s32[]{:S(2)}) async-start(s8[8388608]{0:T(1024)(128)(4,1)} %bitcast.384), calls=%async_computation.17 | async-start | bytes 8388608
  344.1 8.2 %slice-start.14 = ((s8[8388608]{0:T(1024)(128)(4,1)}), s8[4194304]{0:T(1024)(128)(4,1)S(1)}, s32[]{:S(2)}) async-start(s8[8388608]{0:T(1024)(128)(4,1)} %bitcast.390), calls=%async_computation.23 | async-start | bytes 8388608
  391.5 37.7 %copy-start.1 = (bf16[48,128,128]{2,1,0:T(8,128)(2,1)S(1)}, bf16[48,128,128]{2,1,0:T(8,128)(2,1)}, u32[]{:S(2)}) copy-start(bf16[48,128,128]{2,1,0:T(8,128)(2,1)} %param.9) | copy-start | bytes 4718596
  (81 other events, 193.9 us)
Sparse Core Ops, SparseCore 0:
  114.2 21.6 all-gather.7
  137.4 28.4 all-gather.9
  167.5 22.5 all-gather.11
  191.5 22.5 all-gather.15
  215.5 22.5 all-gather.13
  239.6 22.5 all-gather.17
  263.7 22.5 all-gather.19
  394.1 33.7 all-reduce.1
where the time goes:
time: 440 us; the launch traced here: 436 us
  waiting for transfers between devices  180 us (41%)
  matrix products  179 us (41%)
  local copies, waits for them, and re-layouts  30.9 us (7%)
  between operations  19 us (4%)
  starting transfers between devices  16.8 us (4%)
  other arithmetic  10.3 us (2%)
    all_to_all x1, waiting for transfers between devices, body(): lax.all_to_all(outgoing, 'ka', split_axis=0, concat_axis=0, tiled=True)  88.6 us
    dot_general x24, matrix products, density_term(): lax.dot_general(stacked, column_rows, (((1,), (1,)), ((), ())), preferred...  71.7 us
    dot_general x24, matrix products, density_term(): lax.dot_general(left_screen, right_screen[col_start:col_end], (((1,), (1,...  57.9 us
    ppermute x5, waiting for transfers between devices, from_behind(): return lax.ppermute(block, axis, route)  56.7 us
    dot_general x24, matrix products, density_term(): jnp.dot(screened, operand, preferred_element_type=jnp.float32)  47.6 us
    psum x1, waiting for transfers between devices, body(): summed = lax.psum(partial_value, 'pt')  33.9 us
    unnamed x182, local copies, waits for them, and re-layouts  14.2 us
    ppermute x5, starting transfers between devices, from_behind(): return lax.ppermute(block, axis, route)  9.08 us
  transfers between devices with their start and end apart: 14, of which 7 were waited for; matrix products, arithmetic and copies ran while one was open for 41% of the time, Pallas kernels for 0%

commit v1 on v0

--- a/solution.py
+++ b/solution.py
@@ -111,7 +111,7 @@
         stacked_x, right_stack, (((0,), (0,)), ((), ())), preferred_element_type=jnp.float32
     )
     rows_out = n_bands // lax.axis_size("pt")
-    summed = lax.psum(partial_value, "pt")
+    summed = jnp.sum(lax.all_gather(partial_value, "pt"), axis=0)
     kept = lax.dynamic_slice_in_dim(summed, lax.axis_index("pt") * rows_out, rows_out, 0)
     scale_factor = 1.0 / (4.0 * NPTS * math.sqrt(NB))
     kept = kept * scale_factor

time: 440 us -> 412 us (0.936)
  waiting for transfers between devices: 180 us -> 147 us
  blocking collectives: 0 us -> 7.34 us
    psum x1 -> x0, waiting for transfers between devices: 33.9 us -> none  [body(): summed = lax.psum(partial_value, 'pt')]
    all_gather x0 -> x1, blocking collectives: none -> 7.34 us  [body(): summed = jnp.sum(lax.all_gather(partial_value, 'pt'), axis=0)]
  transfers between devices with their start and end apart: 14 -> 13, of which waited for: 7 -> 6; matrix products, arithmetic and copies ran while one was open for 41% -> 44% of each run, Pallas kernels for 0% -> 0%
where the time goes in v1:
time: 412 us; the launch traced here: 408 us
  matrix products  179 us (43%)
  waiting for transfers between devices  147 us (36%)
  local copies, waits for them, and re-layouts  30.7 us (7%)
  between operations  18.7 us (5%)
  starting transfers between devices  16.8 us (4%)
  other arithmetic  9.58 us (2%)
  blocking collectives  7.34 us (2%)
    all_to_all x1, waiting for transfers between devices, body(): lax.all_to_all(outgoing, 'ka', split_axis=0, concat_axis=0, tiled=True)  89 us
    dot_general x24, matrix products, density_term(): lax.dot_general(stacked, column_rows, (((1,), (1,)), ((), ())), preferred...  71.6 us
    dot_general x24, matrix products, density_term(): lax.dot_general(left_screen, right_screen[col_start:col_end], (((1,), (1,...  57.9 us
    ppermute x5, waiting for transfers between devices, from_behind(): return lax.ppermute(block, axis, route)  56.8 us
    dot_general x24, matrix products, density_term(): jnp.dot(screened, operand, preferred_element_type=jnp.float32)  47.6 us
    unnamed x182, local copies, waits for them, and re-layouts  14.1 us
    ppermute x5, starting transfers between devices, from_behind(): return lax.ppermute(block, axis, route)  9.14 us
    squeeze x6, local copies, waits for them, and re-layouts, density_term(): full_block[0, col_start:col_end]  8.67 us
  transfers between devices with their start and end apart: 13, of which 6 were waited for; matrix products, arithmetic and copies ran while one was open for 44% of the time, Pallas kernels for 0%

profile of v1, /device:TPU:0, one launch (start us, length us, event | category | flops | bytes accessed | tf_op | source)
XLA Modules:
  0.0 408.3 jit_solution(12650494155937283890)
XLA Ops:
  11.1 7.4 %all-to-all-start = ((bf16[8,2,1024,128]{3,2,1,0:T(8,128)(2,1)}), bf16[8,2,1024,128]{3,2,1,0:T(8,128)(2,1)}, u32[]{:S(2)}, u32[]{:S(2)}) async-start(bf16[8,2,1024,128]{3,2,1,0:T(8,128)(2,1)} %broadcast_select_fusion), calls=%async_computation | async-start | bytes 8388608 | tf_op jit(solution)/shard_map/all_to_all | solution.py:77
  22.9 89.0 %all-to-all-done = bf16[8,2,1024,128]{3,2,1,0:T(8,128)(2,1)} async-done(((bf16[8,2,1024,128]{3,2,1,0:T(8,128)(2,1)}), bf16[8,2,1024,128]{3,2,1,0:T(8,128)(2,1)}, u32[]{:S(2)}, u32[]{:S(2)}) %all-to-all-start) | async-done | bytes 4194336 | tf_op jit(solution)/shard_map/all_to_all | solution.py:77
  116.4 14.0 %collective-permute-done = bf16[2,1024,128]{2,1,0:T(8,128)(2,1)S(1)} collective-permute-done((bf16[2,1024,128]{2,1,0:T(8,128)(2,1)}, bf16[2,1024,128]{2,1,0:T(8,128)(2,1)S(1)}, u32[]{:S(2)}, u32[]{:S(2)}) %collective-permute-start) | collective-permute-done | bytes 524320 | tf_op jit(solution)/shard_map/ppermute | solution.py:16
  132.2 11.0 %collective-permute-done.2 = bf16[2,1024,128]{2,1,0:T(8,128)(2,1)S(1)} collective-permute-done((bf16[2,1024,128]{2,1,0:T(8,128)(2,1)}, bf16[2,1024,128]{2,1,0:T(8,128)(2,1)S(1)}, u32[]{:S(2)}, u32[]{:S(2)}) %collective-permute-start.2) | collective-permute-done | bytes 524320 | tf_op jit(solution)/shard_map/ppermute | solution.py:16
  144.7 15.2 %collective-permute-done.1 = bf16[2,1024,128]{2,1,0:T(8,128)(2,1)S(1)} collective-permute-done((bf16[2,1024,128]{2,1,0:T(8,128)(2,1)}, bf16[2,1024,128]{2,1,0:T(8,128)(2,1)S(1)}, u32[]{:S(2)}, u32[]{:S(2)}) %collective-permute-start.1) | collective-permute-done | bytes 524320 | tf_op jit(solution)/shard_map/ppermute | solution.py:16
  162.6 10.1 %collective-permute-done.3 = bf16[2,1024,128]{2,1,0:T(8,128)(2,1)S(1)} collective-permute-done((bf16[2,1024,128]{2,1,0:T(8,128)(2,1)}, bf16[2,1024,128]{2,1,0:T(8,128)(2,1)S(1)}, u32[]{:S(2)}, u32[]{:S(2)}) %collective-permute-start.3) | collective-permute-done | bytes 524320 | tf_op jit(solution)/shard_map/ppermute | solution.py:16
  182.3 6.5 %collective-permute-done.4 = bf16[2,1024,128]{2,1,0:T(8,128)(2,1)S(1)} collective-permute-done((bf16[2,1024,128]{2,1,0:T(8,128)(2,1)S(1)}, bf16[2,1024,128]{2,1,0:T(8,128)(2,1)S(1)}, u32[]{:S(2)}, u32[]{:S(2)}) %collective-permute-start.4) | collective-permute-done | bytes 524320 | tf_op jit(solution)/shard_map/ppermute | solution.py:16
  196.3 4.7 %fusion.232 = f32[2048,1024]{0,1:T(8,128)} fusion(bf16[1024,128]{1,0:T(8,128)(2,1)S(1)} %get-tuple-element.101, bf16[1024,128]{1,0:T(8,128)(2,1)S(1)} %get-tuple-element.102, bf16[1024,128]{1,0:T(8,128)(2,1)S(1)} %get-tuple-element.127, bf16[1024,128]{1,0:T(8,128)(2,1)S(1)} %get-tuple-element.128, bf16[1024,128]{1,0:T(8,128)(2,1)S(1)} %get-tuple-element.126), kind=kOutput, calls=%fused_computation.259 | convolution fusion | flops 1078984704 | bytes 9699328 | tf_op jit(solution)/shard_map/dot_general | solution.py:33
  201.0 4.6 %fusion.236 = f32[2048,1024]{0,1:T(8,128)} fusion(bf16[1024,128]{1,0:T(8,128)(2,1)S(1)} %get-tuple-element.99, bf16[1024,128]{1,0:T(8,128)(2,1)S(1)} %get-tuple-element.100, bf16[1024,128]{1,0:T(8,128)(2,1)S(1)} %get-tuple-element.127, bf16[1024,128]{1,0:T(8,128)(2,1)S(1)} %get-tuple-element.128, bf16[1024,128]{1,0:T(8,128)(2,1)S(1)} %get-tuple-element.126), kind=kOutput, calls=%fused_computation.263 | convolution fusion | flops 1078984704 | bytes 9699328 | tf_op jit(solution)/shard_map/dot_general | solution.py:33
  205.6 4.7 %fusion.240 = f32[2048,1024]{0,1:T(8,128)} fusion(bf16[1024,128]{1,0:T(8,128)(2,1)S(1)} %get-tuple-element.97, bf16[1024,128]{1,0:T(8,128)(2,1)S(1)} %get-tuple-element.98, bf16[1024,128]{1,0:T(8,128)(2,1)S(1)} %get-tuple-element.127, bf16[1024,128]{1,0:T(8,128)(2,1)S(1)} %get-tuple-element.128, bf16[1024,128]{1,0:T(8,128)(2,1)S(1)} %get-tuple-element.126), kind=kOutput, calls=%fused_computation.267 | convolution fusion | flops 1078984704 | bytes 9699328 | tf_op jit(solution)/shard_map/dot_general | solution.py:33
  210.3 4.5 %fusion.244 = f32[2048,1024]{0,1:T(8,128)} fusion(bf16[1024,128]{1,0:T(8,128)(2,1)S(1)} %get-tuple-element.96, bf16[1024,128]{1,0:T(8,128)(2,1)S(1)} %get-tuple-element.95, bf16[1024,128]{1,0:T(8,128)(2,1)S(1)} %get-tuple-element.127, bf16[1024,128]{1,0:T(8,128)(2,1)S(1)} %get-tuple-element.128, bf16[1024,128]{1,0:T(8,128)(2,1)S(1)} %get-tuple-element.126), kind=kOutput, calls=%fused_computation.271 | convolution fusion | flops 1078984704 | bytes 9699328 | tf_op jit(solution)/shard_map/dot_general | solution.py:33
  214.9 4.4 %fusion.47 = (bf16[1024,1024]{0,1:T(8,128)(2,1)S(1)}, bf16[1024,1024]{0,1:T(8,128)(2,1)S(1)}) fusion(f32[2048,1024]{0,1:T(8,128)} %fusion.232, bf16[6,4096,64]{1,2,0:T(8,128)(2,1)} %all-gather.11.cloned.1.call-done, bf16[6,1024,64]{1,2,0:T(8,128)(2,1)S(1)} %copy-done.3), kind=kOutput, calls=%fused_computation.95 | convolution fusion | flops 138412032 | bytes 12845056 | tf_op jit(solution)/shard_map/dot_general | solution.py:36
  241.7 4.7 %fusion.252 = f32[2048,1024]{0,1:T(8,128)} fusion(bf16[1024,128]{1,0:T(8,128)(2,1)S(1)} %get-tuple-element.91, bf16[1024,128]{1,0:T(8,128)(2,1)S(1)} %get-tuple-element.92, bf16[1024,128]{1,0:T(8,128)(2,1)S(1)} %fusion.453, bf16[1024,128]{1,0:T(8,128)(2,1)S(1)} %copy-done.14, bf16[1024,128]{1,0:T(8,128)(2,1)S(1)} %copy-done.13), kind=kOutput, calls=%fused_computation.279 | convolution fusion | flops 1078984704 | bytes 9699328 | tf_op jit(solution)/shard_map/dot_general | solution.py:33
  246.4 4.6 %fusion.256 = f32[2048,1024]{0,1:T(8,128)} fusion(bf16[1024,128]{1,0:T(8,128)(2,1)S(1)} %get-tuple-element.89, bf16[1024,128]{1,0:T(8,128)(2,1)S(1)} %get-tuple-element.90, bf16[1024,128]{1,0:T(8,128)(2,1)S(1)} %fusion.453, bf16[1024,128]{1,0:T(8,128)(2,1)S(1)} %copy-done.14, bf16[1024,128]{1,0:T(8,128)(2,1)S(1)} %copy-done.13), kind=kOutput, calls=%fused_computation.283 | convolution fusion | flops 1078984704 | bytes 9699328 | tf_op jit(solution)/shard_map/dot_general | solution.py:33
  251.0 4.7 %fusion.260 = f32[2048,1024]{0,1:T(8,128)} fusion(bf16[1024,128]{1,0:T(8,128)(2,1)S(1)} %get-tuple-element.88, bf16[1024,128]{1,0:T(8,128)(2,1)S(1)} %get-tuple-element.87, bf16[1024,128]{1,0:T(8,128)(2,1)S(1)} %fusion.453, bf16[1024,128]{1,0:T(8,128)(2,1)S(1)} %copy-done.14, bf16[1024,128]{1,0:T(8,128)(2,1)S(1)} %copy-done.13), kind=kOutput, calls=%fused_computation.287 | convolution fusion | flops 1078984704 | bytes 9699328 | tf_op jit(solution)/shard_map/dot_general | solution.py:33
  271.9 5.2 %fusion.203 = f32[1024,256]{1,0:T(8,128)} fusion(f32[1024,256]{1,0:T(8,128)} %fusion.64, bf16[1024,1024]{0,1:T(8,128)(2,1)} %get-tuple-element.44, bf16[1024,1024]{0,1:T(8,128)(2,1)} %get-tuple-element.43, bf16[1024,256]{1,0:T(8,128)(2,1)} %get-tuple-element.111, bf16[1024,256]{1,0:T(8,128)(2,1)} %get-tuple-element.105), kind=kOutput, calls=%fused_computation.228 | convolution fusion | flops 1084489728 | bytes 7340032 | tf_op jit(solution)/shard_map/dot_general | solution.py:48
  304.4 4.6 %fusion.268 = f32[2048,1024]{0,1:T(8,128)} fusion(bf16[1024,128]{1,0:T(8,128)(2,1)S(1)} %get-tuple-element.83, bf16[1024,128]{1,0:T(8,128)(2,1)S(1)} %get-tuple-element.84, bf16[1024,128]{1,0:T(8,128)(2,1)S(1)} %fusion.454, bf16[1024,128]{1,0:T(8,128)(2,1)S(1)} %copy-done.9, bf16[1024,128]{1,0:T(8,128)(2,1)S(1)} %copy-done.8), kind=kOutput, calls=%fused_computation.295 | convolution fusion | flops 1078984704 | bytes 9699328 | tf_op jit(solution)/shard_map/dot_general | solution.py:33
  308.9 4.7 %fusion.272 = f32[2048,1024]{0,1:T(8,128)} fusion(bf16[1024,128]{1,0:T(8,128)(2,1)S(1)} %get-tuple-element.81, bf16[1024,128]{1,0:T(8,128)(2,1)S(1)} %get-tuple-element.82, bf16[1024,128]{1,0:T(8,128)(2,1)S(1)} %fusion.454, bf16[1024,128]{1,0:T(8,128)(2,1)S(1)} %copy-done.9, bf16[1024,128]{1,0:T(8,128)(2,1)S(1)} %copy-done.8), kind=kOutput, calls=%fused_computation.299 | convolution fusion | flops 1078984704 | bytes 9699328 | tf_op jit(solution)/shard_map/dot_general | solution.py:33
  313.6 4.6 %fusion.276 = f32[2048,1024]{0,1:T(8,128)} fusion(bf16[1024,128]{1,0:T(8,128)(2,1)S(1)} %get-tuple-element.80, bf16[1024,128]{1,0:T(8,128)(2,1)S(1)} %get-tuple-element.79, bf16[1024,128]{1,0:T(8,128)(2,1)S(1)} %fusion.454, bf16[1024,128]{1,0:T(8,128)(2,1)S(1)} %copy-done.9, bf16[1024,128]{1,0:T(8,128)(2,1)S(1)} %copy-done.8), kind=kOutput, calls=%fused_computation.303 | convolution fusion | flops 1078984704 | bytes 9699328 | tf_op jit(solution)/shard_map/dot_general | solution.py:33
  319.9 4.7 %fusion.296 = f32[2048,1024]{0,1:T(8,128)} fusion(bf16[1024,128]{1,0:T(8,128)(2,1)S(1)} %get-tuple-element.69, bf16[1024,128]{1,0:T(8,128)(2,1)S(1)} %get-tuple-element.70, bf16[1024,128]{1,0:T(8,128)(2,1)S(1)} %fusion.456, bf16[1024,128]{1,0:T(8,128)(2,1)S(1)} %copy-done.7, bf16[1024,128]{1,0:T(8,128)(2,1)S(1)} %get-tuple-element.118), kind=kOutput, calls=%fused_computation.323 | convolution fusion | flops 1078984704 | bytes 9699328 | tf_op jit(solution)/shard_map/dot_general | solution.py:33
  324.6 4.7 %fusion.300 = f32[2048,1024]{0,1:T(8,128)} fusion(bf16[1024,128]{1,0:T(8,128)(2,1)S(1)} %get-tuple-element.67, bf16[1024,128]{1,0:T(8,128)(2,1)S(1)} %get-tuple-element.68, bf16[1024,128]{1,0:T(8,128)(2,1)S(1)} %fusion.456, bf16[1024,128]{1,0:T(8,128)(2,1)S(1)} %copy-done.7, bf16[1024,128]{1,0:T(8,128)(2,1)S(1)} %get-tuple-element.118), kind=kOutput, calls=%fused_computation.327 | convolution fusion | flops 1078984704 | bytes 9699328 | tf_op jit(solution)/shard_map/dot_general | solution.py:33
  337.0 5.2 %fusion.191 = f32[1024,256]{1,0:T(8,128)} fusion(f32[1024,256]{1,0:T(8,128)} %fusion.80, bf16[1024,1024]{0,1:T(8,128)(2,1)} %get-tuple-element.36, bf16[1024,1024]{0,1:T(8,128)(2,1)} %get-tuple-element.35, bf16[1024,256]{1,0:T(8,128)(2,1)} %get-tuple-element.111, bf16[1024,256]{1,0:T(8,128)(2,1)} %get-tuple-element.105), kind=kOutput, calls=%fused_computation.224 | convolution fusion | flops 1084489728 | bytes 7340032 | tf_op jit(solution)/shard_map/dot_general | solution.py:48
  345.7 6.4 %fusion.15 = (bf16[1024,1024]{0,1:T(8,128)(2,1)}, bf16[1024,1024]{0,1:T(8,128)(2,1)}) fusion(f32[2048,1024]{0,1:T(8,128)} %fusion.296, bf16[6,4096,64]{1,2,0:T(8,128)(2,1)} %all-gather.11.cloned.1.call-done, bf16[6,1024,64]{1,2,0:T(8,128)(2,1)S(1)} %copy-done.3), kind=kOutput, calls=%fused_computation.31 | convolution fusion | flops 138412032 | bytes 12845056 | tf_op jit(solution)/shard_map/dot_general | solution.py:36
  393.2 7.3 %all-gather = f32[512,256]{1,0:T(8,128)S(1)} all-gather(f32[128,256]{1,0:T(8,128)S(1)} %fusion.220), channel_id=2, replica_groups=mesh['ka'=8,'pt'=4] {'pt'}, dimensions={0}, use_global_device_ids=true | all-gather | bytes 655360 | tf_op jit(solution)/shard_map/all_gather | solution.py:114
  (307 shorter events, 152.2 us)
Async XLA Ops:
  6.5 106.4 %copy-start = (bf16[48,128,128]{2,1,0:T(8,128)(2,1)S(1)}, bf16[48,128,128]{2,1,0:T(8,128)(2,1)}, u32[]{:S(2)}) copy-start(bf16[48,128,128]{2,1,0:T(8,128)(2,1)} %param.9) | copy-start | bytes 4718596
  11.1 7.5 %copy-start.63 = (s32[8,4]{0,1:T(4,128)S(1)}, s32[8,4]{0,1:T(4,128)}, u32[]{:S(2)}) copy-start(s32[8,4]{0,1:T(4,128)} %param.7) | copy-start | bytes 388
  11.1 7.5 %copy-start.64 = (s32[8,4]{0,1:T(4,128)S(1)}, s32[8,4]{0,1:T(4,128)}, u32[]{:S(2)}) copy-start(s32[8,4]{0,1:T(4,128)} %param.8) | copy-start | bytes 388
  11.1 100.7 %all-to-all-start = ((bf16[8,2,1024,128]{3,2,1,0:T(8,128)(2,1)}), bf16[8,2,1024,128]{3,2,1,0:T(8,128)(2,1)}, u32[]{:S(2)}, u32[]{:S(2)}) async-start(bf16[8,2,1024,128]{3,2,1,0:T(8,128)(2,1)} %broadcast_select_fusion), calls=%async_computation | async-start | bytes 8388608 | tf_op jit(solution)/shard_map/all_to_all | solution.py:77
  18.6 171.8 %all-gather.9.cloned.1.call-start = ((), (), s32[]{:S(2)}) async-start(), calls=%async_computation.1 | async-start | bytes 2621440 | tf_op jit(solution)/shard_map/all_gather | solution.py:81
  114.0 59.6 %copy-start.15 = (bf16[2048,128]{1,0:T(8,128)(2,1)S(1)}, bf16[2048,128]{1,0:T(8,128)(2,1)}, u32[]{:S(2)}) copy-start(bf16[2048,128]{1,0:T(8,128)(2,1)} %convolution_convert_fusion) | copy-start | bytes 1572868
  114.0 100.8 %all-gather.11.cloned.1.call-start = ((), (), s32[]{:S(2)}) async-start(), calls=%async_computation.2 | async-start | bytes 3932160 | tf_op jit(solution)/shard_map/all_gather | solution.py:82
  114.8 119.9 %all-gather.13.cloned.1.call-start = ((), (), s32[]{:S(2)}) async-start(), calls=%async_computation.3 | async-start | bytes 2621440 | tf_op jit(solution)/shard_map/all_gather | solution.py:94
  114.8 15.5 %collective-permute-start = (bf16[2,1024,128]{2,1,0:T(8,128)(2,1)}, bf16[2,1024,128]{2,1,0:T(8,128)(2,1)S(1)}, u32[]{:S(2)}, u32[]{:S(2)}) collective-permute-start(bf16[2,1024,128]{2,1,0:T(8,128)(2,1)} %bitcast.396), channel_id=1, source_target_pairs={{28,0},{0,4},{4,8},{8,12},{12,16},{16,20},{20,24},{24,28},{29,1},{... | collective-permute-start | bytes 1572872 | tf_op jit(solution)/shard_map/ppermute | solution.py:16
  131.2 42.5 %copy-start.25 = (bf16[2,1024,128]{2,1,0:T(8,128)(2,1)S(1)}, bf16[2,1024,128]{2,1,0:T(8,128)(2,1)}, u32[]{:S(2)}) copy-start(bf16[2,1024,128]{2,1,0:T(8,128)(2,1)} %copy-done.24) | copy-start | bytes 1572868
  131.2 124.5 %all-gather.17.cloned.1.call-start = ((), (), s32[]{:S(2)}) async-start(), calls=%async_computation.5 | async-start | bytes 2621440 | tf_op jit(solution)/shard_map/all_gather | solution.py:94
  131.2 12.0 %collective-permute-start.2 = (bf16[2,1024,128]{2,1,0:T(8,128)(2,1)}, bf16[2,1024,128]{2,1,0:T(8,128)(2,1)S(1)}, u32[]{:S(2)}, u32[]{:S(2)}) collective-permute-start(bf16[2,1024,128]{2,1,0:T(8,128)(2,1)} %bitcast.397), channel_id=1, source_target_pairs={{4,0},{8,4},{12,8},{16,12},{20,16},{24,20},{28,24},{0,28},{5,1},{9... | collective-permute-start | bytes 1572872 | tf_op jit(solution)/shard_map/ppermute | solution.py:16
  144.1 29.7 %copy-start.23 = (bf16[2,1024,128]{2,1,0:T(8,128)(2,1)S(1)}, bf16[2,1024,128]{2,1,0:T(8,128)(2,1)}, u32[]{:S(2)}) copy-start(bf16[2,1024,128]{2,1,0:T(8,128)(2,1)} %copy-done.22) | copy-start | bytes 1572868
  144.1 153.2 %all-gather.15.cloned.1.call-start = ((), (), s32[]{:S(2)}) async-start(), calls=%async_computation.4 | async-start | bytes 2621440 | tf_op jit(solution)/shard_map/all_gather | solution.py:94
  144.1 15.8 %collective-permute-start.1 = (bf16[2,1024,128]{2,1,0:T(8,128)(2,1)}, bf16[2,1024,128]{2,1,0:T(8,128)(2,1)S(1)}, u32[]{:S(2)}, u32[]{:S(2)}) collective-permute-start(bf16[2,1024,128]{2,1,0:T(8,128)(2,1)} %copy-done.24), channel_id=1, source_target_pairs={{28,0},{0,4},{4,8},{8,12},{12,16},{16,20},{20,24},{24,28},{29,1},{... | collective-permute-start | bytes 1572872 | tf_op jit(solution)/shard_map/ppermute | solution.py:16
  160.7 157.5 %all-gather.19.cloned.1.call-start = ((), (), s32[]{:S(2)}) async-start(), calls=%async_computation.6 | async-start | bytes 2621440 | tf_op jit(solution)/shard_map/all_gather | solution.py:94
  160.8 11.9 %collective-permute-start.3 = (bf16[2,1024,128]{2,1,0:T(8,128)(2,1)}, bf16[2,1024,128]{2,1,0:T(8,128)(2,1)S(1)}, u32[]{:S(2)}, u32[]{:S(2)}) collective-permute-start(bf16[2,1024,128]{2,1,0:T(8,128)(2,1)} %copy-done.22), channel_id=1, source_target_pairs={{4,0},{8,4},{12,8},{16,12},{20,16},{24,20},{28,24},{0,28},{5,1},{9... | collective-permute-start | bytes 1572872 | tf_op jit(solution)/shard_map/ppermute | solution.py:16
  173.5 199.7 %all-gather.21.cloned.1.call-start = ((), (), s32[]{:S(2)}) async-start(), calls=%async_computation.7 | async-start | bytes 2621440 | tf_op jit(solution)/shard_map/all_gather | solution.py:94
  176.3 12.4 %collective-permute-start.4 = (bf16[2,1024,128]{2,1,0:T(8,128)(2,1)S(1)}, bf16[2,1024,128]{2,1,0:T(8,128)(2,1)S(1)}, u32[]{:S(2)}, u32[]{:S(2)}) collective-permute-start(bf16[2,1024,128]{2,1,0:T(8,128)(2,1)S(1)} %copy-done.19), channel_id=1, source_target_pairs={{4,0},{8,4},{12,8},{16,12},{20,16},{24,20},{28,24},{0,28},{5,1},{9... | collective-permute-start | bytes 1572872 | tf_op jit(solution)/shard_map/ppermute | solution.py:16
  268.1 9.1 %slice-start.2 = ((s8[8388608]{0:T(1024)(128)(4,1)}), s8[4194304]{0:T(1024)(128)(4,1)S(1)}, s32[]{:S(2)}) async-start(s8[8388608]{0:T(1024)(128)(4,1)} %bitcast.377), calls=%async_computation.10 | async-start | bytes 8388608
  333.0 9.2 %slice-start.6 = ((s8[8388608]{0:T(1024)(128)(4,1)}), s8[4194304]{0:T(1024)(128)(4,1)S(1)}, s32[]{:S(2)}) async-start(s8[8388608]{0:T(1024)(128)(4,1)} %bitcast.381), calls=%async_computation.14 | async-start | bytes 8388608
  333.0 10.8 %slice-start.8 = ((s8[8388608]{0:T(1024)(128)(4,1)}), s8[4194304]{0:T(1024)(128)(4,1)S(1)}, s32[]{:S(2)}) async-start(s8[8388608]{0:T(1024)(128)(4,1)} %bitcast.383), calls=%async_computation.16 | async-start | bytes 8388608
  343.9 8.3 %slice-start.14 = ((s8[8388608]{0:T(1024)(128)(4,1)}), s8[4194304]{0:T(1024)(128)(4,1)S(1)}, s32[]{:S(2)}) async-start(s8[8388608]{0:T(1024)(128)(4,1)} %bitcast.389), calls=%async_computation.22 | async-start | bytes 8388608
  392.8 8.4 %copy-start.1 = (bf16[48,128,128]{2,1,0:T(8,128)(2,1)S(1)}, bf16[48,128,128]{2,1,0:T(8,128)(2,1)}, u32[]{:S(2)}) copy-start(bf16[48,128,128]{2,1,0:T(8,128)(2,1)} %param.9) | copy-start | bytes 4718596
  (80 other events, 186.0 us)
Sparse Core Ops, SparseCore 0:
  114.2 21.6 all-gather.8
  137.4 28.4 all-gather.10
  167.5 22.5 all-gather.12
  191.5 22.5 all-gather.16
  215.5 22.5 all-gather.14
  239.5 22.5 all-gather.18
  263.7 22.5 all-gather.20
